TPU v7x, 256 devices: a whole 4x4x8 slice. The times are simulated.
256 devices in a mesh: tile: 64 (over z, y, x_lo), rot: 4 (over x_hi, core).
Axes of the slice: x: 4 (x_hi: 2, x_lo: 2; x = x_hi * 2 + x_lo), y: 4, z: 8, core: 2. Of those that a mesh axis runs over, the one named last changes fastest.
Arguments:
- tomogram: bfloat16 [1024, 128, 128], P('tile'), may hold values from -6 to 6
- templates: bfloat16 [64, 32, 32, 32], P('tile'), may hold values from -6 to 6
- owners: int32 [1], replicated, may hold values from 0 to 63
- orient_ids: int32 [1, 4], P(None, 'rot'), may hold values from 0 to 23
- slice_mask: int32 [1024], P('tile'), may hold values 0 or 1
Outputs:
- best_score: float32 [1024, 128, 128], P('tile')
All inputs are finite; a program needn't handle non-finite values. No bound on the sum of `slice_mask` on one device may be relied on, other than what follows from the above.
Results may differ from a plain program's by a relative error of at most 0.012.
Values may be sent and summed in bfloat16 or wider, within the bound.
No kernel may reach another device: no remote copies, remote signals or barrier semaphores. Data moves between devices by JAX's collectives and lax.ppermute only.
A program may use at most 64 MiB of HBM per device.

v0:
```python
import itertools
import math

import jax
import jax.numpy as jnp
import numpy as np
from jax import lax
from jax.experimental import pallas as pl
from jax.experimental.pallas import tpu as pltpu
from jax.sharding import Mesh
from jax.sharding import PartitionSpec as P


TILE = ("tile_0", "tile_1", "tile_2")
EDGE = 32
SLAB = 16
WIDE = 128
LENGTH = 48
HALF = LENGTH // 2
FREQS = HALF + 1
PAIRS = (FREQS + 1) // 2
BF16 = jnp.bfloat16
F32 = jnp.float32


def plus(a, b):
    if a is None:
        return b
    return a if b is None else a + b


def minus(a, b):
    if b is None:
        return a
    return -b if a is None else a - b


def weighted(terms):
    total = None
    for value, weight in terms:
        if value is None or abs(weight) < 1e-9:
            continue
        if abs(abs(weight) - 1.0) < 1e-9:
            part = value
        else:
            part = value * jnp.float32(abs(weight))
        if weight > 0:
            total = plus(total, part)
        else:
            total = minus(total, part)
    return total


def cosine(j, k, n):
    return math.cos(2.0 * math.pi * ((j * k) % n) / n)


def sine(j, k, n):
    return math.sin(2.0 * math.pi * ((j * k) % n) / n)


def cos_forward(n, e):
    half = n // 2
    if n % 4:
        return [weighted([(e[j], cosine(j, k, n)) for j in range(half + 1)]) for k in range(half + 1)]
    even = cos_forward(half, e[0::2])
    out = [None] * (half + 1)
    for k in range(n // 4 + 1):
        odd = weighted([(e[j], cosine(j, k, n)) for j in range(1, half, 2)])
        out[k] = plus(even[k], odd)
        if k < n // 4:
            out[half - k] = minus(even[k], odd)
    return out


def sin_forward(n, o):
    half = n // 2
    if n % 4:
        return [weighted([(o[j], sine(j, k, n)) for j in range(1, half)]) if k % half else None for k in range(half + 1)]
    even = sin_forward(half, o[0::2])
    out = [None] * (half + 1)
    for k in range(1, n // 4 + 1):
        odd = weighted([(o[j], sine(j, k, n)) for j in range(1, half, 2)])
        out[k] = plus(even[k], odd) if k < n // 4 else odd
        if k < n // 4:
            out[half - k] = minus(odd, even[k])
    return out


def cos_inverse(n, f, wanted):
    half, quarter = n // 2, n // 4
    if n % 4:
        return {x: weighted([(f[k], cosine(k, x, n)) for k in range(half + 1)]) for x in wanted}
    out = {}
    evens = [x // 2 for x in wanted if x % 2 == 0]
    odds = [x for x in wanted if x % 2]
    if odds:
        q = [minus(f[k], f[half - k]) for k in range(quarter)]
        for x in odds:
            out[x] = weighted([(q[k], cosine(k, x, n)) for k in range(quarter)])
    if evens:
        p = [plus(f[k], f[half - k]) for k in range(quarter)] + [f[quarter]]
        for x, value in cos_inverse(half, p, evens).items():
            out[2 * x] = value
    return out


def sin_inverse(n, g, wanted):
    half, quarter = n // 2, n // 4
    if n % 4:
        return {x: weighted([(g[k], sine(k, x, n)) for k in range(1, half)]) for x in wanted}
    out = {}
    evens = [x // 2 for x in wanted if x % 2 == 0]
    odds = [x for x in wanted if x % 2]
    if odds:
        t = [None] + [plus(g[k], g[half - k]) for k in range(1, quarter)] + [g[quarter]]
        for x in odds:
            out[x] = weighted([(t[k], sine(k, x, n)) for k in range(1, quarter + 1)])
    if evens:
        r = [None] + [minus(g[k], g[half - k]) for k in range(1, quarter)] + [None]
        for x, value in sin_inverse(half, r, evens).items():
            out[2 * x] = value
    return out


def slices_forward(s):
    e = [s[0]] + [plus(s[j], s[LENGTH - j]) for j in range(1, HALF)] + [s[HALF]]
    o = [None] + [minus(s[j], s[LENGTH - j]) for j in range(1, HALF)] + [None]
    return cos_forward(LENGTH, e), sin_forward(LENGTH, o)


def tables():
    def table(rows, cols):
        angle = (np.outer(np.arange(rows), np.arange(cols)) % WIDE).astype(np.float32)
        angle = angle * np.float32(2.0 * math.pi / WIDE)
        return np.cos(angle), np.sin(angle)

    c, s = table(WIDE, WIDE)
    first = np.block([[c, -s], [s, c]])
    second = np.block([[c, s], [-s, c]])
    small_z, small_y = [], []
    for flip in (False, True):
        c, s = table(EDGE, WIDE)
        if flip:
            c, s = c[::-1], s[::-1]
        small_z.append(np.block([[c, -s], [s, c]]))
        small_y.append(np.block([[c.T, s.T], [-s.T, c.T]]))
    return [
        jnp.asarray(t.astype(np.float32)).astype(BF16)
        for t in (first, second, np.stack(small_z), np.stack(small_y))
    ]


def dot(a, b):
    return jnp.dot(a, b, preferred_element_type=F32)


def spot(k):
    return k // 2, (k % 2) * WIDE


def fill_halo(core_ref, own_ref, other_ref, halo_ref):
    core = core_ref[0]
    for hop in range(2):
        halo_ref[pl.ds(hop * SLAB + 8 * core, 8)] = own_ref[hop]
        halo_ref[pl.ds(hop * SLAB + 8 * (1 - core), 8)] = other_ref[hop]


def load_rows(tomo_ref, halo_ref, at):
    s = [tomo_ref[j, at, :] if j < SLAB else halo_ref[j - SLAB, at, :] for j in range(LENGTH - 1)]
    return [value.astype(F32) for value in s]


def spectrum_kernel(core_ref, tomo_ref, own_ref, other_ref, first_ref, second_ref, spec_ref,
                    halo_ref, x_ref, z_ref):
    fill_halo(core_ref, own_ref, other_ref, halo_ref)

    def rows(step, carry):
        at = pl.ds(pl.multiple_of(step * 16, 16), 16)
        real, imag = slices_forward(load_rows(tomo_ref, halo_ref, at) + [None])
        for k in range(FREQS):
            x_ref[k, at, :WIDE] = real[k].astype(BF16)
            if imag[k] is None:
                x_ref[k, at, WIDE:] = jnp.zeros((16, WIDE), BF16)
            else:
                x_ref[k, at, WIDE:] = (-imag[k]).astype(BF16)
        return carry

    lax.fori_loop(0, WIDE // 16, rows, 0)

    for k in range(FREQS):
        pair, lane = spot(k)
        moved = dot(x_ref[k], first_ref[...]).astype(BF16)
        z_ref[pair, :WIDE, lane:lane + WIDE] = moved[:, :WIDE]
        z_ref[pair, WIDE:, lane:lane + WIDE] = moved[:, WIDE:]
    for pair in range(PAIRS):
        width = WIDE if pair == PAIRS - 1 else 2 * WIDE
        spec_ref[pair, :, :width] = dot(second_ref[...], z_ref[pair, :, :width]).astype(BF16)
        if width == WIDE:
            spec_ref[pair, :, WIDE:] = jnp.zeros((2 * WIDE, WIDE), BF16)


def factor_kernel(core_ref, tomo_ref, own_ref, other_ref, factor_ref, halo_ref, sum_ref, square_ref):
    fill_halo(core_ref, own_ref, other_ref, halo_ref)

    def windows(step, carry):
        at = pl.ds(pl.multiple_of(step * 16, 16), 16)
        s = load_rows(tomo_ref, halo_ref, at)
        for target, field in ((sum_ref, s), (square_ref, [value * value for value in s])):
            for reach in (1, 2, 4, 8, 16):
                field = [field[j] + field[j + reach] for j in range(len(field) - reach)]
            for x in range(SLAB):
                target[x, at, :] = field[x]
        return carry

    lax.fori_loop(0, WIDE // 16, windows, 0)

    volume = float(EDGE**3)

    def boxed(field):
        for axis in (0, 1):
            for reach in (1, 2, 4, 8, 16):
                field = field + pltpu.roll(field, WIDE - reach, axis)
        return field / volume

    def scale(x, carry):
        mean_t = boxed(sum_ref[x])
        mean_sq = boxed(square_ref[x])
        root = lax.rsqrt(mean_sq - mean_t * mean_t + 1e-05) / jnp.float32(math.sqrt(volume))
        factor_ref[x] = root * jnp.float32(2.0 / (LENGTH * WIDE * WIDE))
        return carry

    lax.fori_loop(0, SLAB, scale, 0)


def spectrum_call(core, tomogram, own, other, first, second):
    vmem = pl.BlockSpec(memory_space=pltpu.VMEM)
    return pl.pallas_call(
        spectrum_kernel,
        out_shape=jax.ShapeDtypeStruct((PAIRS, 2 * WIDE, 2 * WIDE), BF16),
        in_specs=[pl.BlockSpec(memory_space=pltpu.SMEM)] + [vmem] * 5,
        out_specs=vmem,
        scratch_shapes=[
            pltpu.VMEM((2 * SLAB, WIDE, WIDE), BF16),
            pltpu.VMEM((FREQS, WIDE, 2 * WIDE), BF16),
            pltpu.VMEM((PAIRS, 2 * WIDE, 2 * WIDE), BF16),
        ],
        compiler_params=pltpu.CompilerParams(vmem_limit_bytes=40 << 20),
        cost_estimate=pl.CostEstimate(flops=4_000_000_000, transcendentals=0, bytes_accessed=6_000_000),
        name="spectrum",
    )(core, tomogram, own, other, first, second)


def factor_call(core, tomogram, own, other):
    vmem = pl.BlockSpec(memory_space=pltpu.VMEM)
    return pl.pallas_call(
        factor_kernel,
        out_shape=jax.ShapeDtypeStruct((SLAB, WIDE, WIDE), F32),
        in_specs=[pl.BlockSpec(memory_space=pltpu.SMEM)] + [vmem] * 3,
        out_specs=vmem,
        scratch_shapes=[
            pltpu.VMEM((2 * SLAB, WIDE, WIDE), BF16),
            pltpu.VMEM((SLAB, WIDE, WIDE), F32),
            pltpu.VMEM((SLAB, WIDE, WIDE), F32),
        ],
        compiler_params=pltpu.CompilerParams(vmem_limit_bytes=40 << 20),
        cost_estimate=pl.CostEstimate(flops=4_000_000_000, transcendentals=0, bytes_accessed=6_000_000),
        name="factor",
    )(core, tomogram, own, other)


def prep_kernel(core_ref, tomo_ref, temp_ref, slices_ref, packed_ref):
    slices_ref[...] = tomo_ref[...]
    values = temp_ref[0].astype(F32).reshape(16 * EDGE, EDGE)
    rows = 4 * EDGE
    packed = jnp.concatenate([values[g * rows:(g + 1) * rows] for g in range(4)], axis=1).astype(BF16)
    for member in range(packed_ref.shape[0]):
        packed_ref[member] = packed


def prep_call(core, tomogram, templates, members):
    return pl.pallas_call(
        prep_kernel,
        out_shape=(
            jax.ShapeDtypeStruct((SLAB // 2, WIDE, WIDE), BF16),
            jax.ShapeDtypeStruct((members, WIDE, WIDE), BF16),
        ),
        grid_spec=pltpu.PrefetchScalarGridSpec(
            num_scalar_prefetch=1,
            grid=(1,),
            in_specs=[
                pl.BlockSpec((SLAB // 2, WIDE, WIDE), lambda i, core: (core[0], 0, 0)),
                pl.BlockSpec((1, EDGE // 2, EDGE, EDGE), lambda i, core: (0, core[0], 0, 0)),
            ],
            out_specs=(
                pl.BlockSpec((SLAB // 2, WIDE, WIDE), lambda i, core: (0, 0, 0)),
                pl.BlockSpec((members, WIDE, WIDE), lambda i, core: (0, 0, 0)),
            ),
        ),
        name="prep",
    )(core, tomogram, templates)


def match_kernel(core_ref, orient_ref, own_ref, other_ref, spec_ref, factor_ref, first_ref, second_ref,
                 small_z_ref, small_y_ref, best_ref,
                 base_ref, cube_ref, cube_out_ref, packed_ref, a_ref, z_ref, p_ref, q_ref, f_ref, held_ref):
    step = pl.program_id(0)
    core = core_ref[0]

    @pl.when(step == 0)
    def _():
        for mine, half_ref in ((core, own_ref), (1 - core, other_ref)):
            values = half_ref[...].astype(F32)
            for group in range(4):
                start = pl.multiple_of((16 * mine + 4 * group) * EDGE, 128)
                base_ref[pl.ds(start, 4 * EDGE), :] = values[:, group * EDGE:(group + 1) * EDGE]
        values = base_ref[...]
        total = float(EDGE**3)
        center = jnp.sum(values) / total
        values = values - center
        spread = jnp.sum(values * values) / total
        base_ref[...] = (values * lax.rsqrt(spread + 1e-05)).astype(BF16).astype(F32)

    index = orient_ref[step]
    order = index // 4
    flips = index % 4
    odd_order = order >= 3
    turn_a = (order == 2) | (order == 3) | (order == 4)
    turn_b = (order == 1) | (order == 2) | (order == 4) | (order == 5)
    turn_c = (order == 1) | (order == 4)
    flip_y = flips % 2
    flip_z = flips // 2
    middle = ((flips == 1) | (flips == 2)).astype(jnp.int32)
    flip_x = jnp.where(odd_order, 1 - middle, middle)

    def swap_last(source, target):
        for a in range(EDGE):
            at = slice(a * EDGE, (a + 1) * EDGE)
            target[at, :] = source[at, :].T

    def copy(source, target):
        target[...] = source[...]

    @pl.when(turn_a)
    def _():
        swap_last(base_ref, cube_ref)

    @pl.when(jnp.logical_not(turn_a))
    def _():
        copy(base_ref, cube_ref)

    @pl.when(turn_b)
    def _():
        for b in range(EDGE):
            cube_out_ref[b * EDGE:(b + 1) * EDGE, :] = cube_ref[pl.ds(b, EDGE, stride=EDGE), :]

    @pl.when(jnp.logical_not(turn_b))
    def _():
        copy(cube_ref, cube_out_ref)

    @pl.when(turn_c)
    def _():
        swap_last(cube_out_ref, cube_ref)

    @pl.when(jnp.logical_not(turn_c))
    def _():
        copy(cube_out_ref, cube_ref)

    for x in range(EDGE):
        tile = cube_ref[x * EDGE:(x + 1) * EDGE, :]
        packed_ref[x] = jnp.concatenate([tile[8 * g:8 * g + 8] for g in range(4)], axis=1)

    s = [None] * LENGTH
    for i in range(EDGE):
        s[i + SLAB // 2] = packed_ref[jnp.where(flip_x == 1, EDGE - 1 - i, i)]
    real, imag = slices_forward(s)
    for k in range(FREQS):
        share = 0.5 if k in (0, HALF) else 1.0
        for g in range(4):
            at = slice(k * EDGE + 8 * g, k * EDGE + 8 * g + 8)
            lanes = slice(g * EDGE, (g + 1) * EDGE)
            a_ref[at, :EDGE] = real[k][:, lanes] * jnp.float32(share)
            if imag[k] is None:
                a_ref[at, EDGE:2 * EDGE] = jnp.zeros((8, EDGE), F32)
            else:
                a_ref[at, EDGE:2 * EDGE] = -imag[k][:, lanes]

    moved = dot(a_ref[...].astype(BF16), small_z_ref[flip_z]).astype(BF16)
    for k in range(FREQS):
        pair, lane = spot(k)
        part = moved[k * EDGE:(k + 1) * EDGE]
        z_ref[pair, :EDGE, lane:lane + WIDE] = part[:, :WIDE]
        z_ref[pair, EDGE:, lane:lane + WIDE] = part[:, WIDE:]

    small_y = small_y_ref[flip_y]
    for pair in range(PAIRS):
        width = WIDE if pair == PAIRS - 1 else 2 * WIDE
        temp = dot(small_y, z_ref[pair, :, :width])
        slab = spec_ref[pair, :, :width].astype(F32)
        temp_r, temp_i = temp[:WIDE], temp[WIDE:]
        slab_r, slab_i = slab[:WIDE], slab[WIDE:]
        prod_r = (slab_r * temp_r + slab_i * temp_i).astype(BF16)
        prod_i = (slab_i * temp_r - slab_r * temp_i).astype(BF16)
        for part in range(width // WIDE):
            k = 2 * pair + part
            lanes = slice(part * WIDE, (part + 1) * WIDE)
            p_ref[k, :, :WIDE] = prod_r[:, lanes]
            p_ref[k, :, WIDE:] = prod_i[:, lanes]

    for k in range(FREQS):
        pair, lane = spot(k)
        moved = dot(p_ref[k], second_ref[...]).astype(BF16)
        q_ref[pair, :WIDE, lane:lane + WIDE] = moved[:, :WIDE]
        q_ref[pair, WIDE:, lane:lane + WIDE] = moved[:, WIDE:]
    for pair in range(PAIRS):
        width = WIDE if pair == PAIRS - 1 else 2 * WIDE
        f_ref[pair, :, :width] = dot(first_ref[...], q_ref[pair, :, :width])

    def scores(block, finish):
        at = pl.multiple_of(block * 8, 8)
        fr, fi = [], []
        for k in range(FREQS):
            pair, lane = spot(k)
            fr.append(f_ref[pair, pl.ds(at, 8), lane:lane + WIDE])
            fi.append(f_ref[pair, pl.ds(WIDE + at, 8), lane:lane + WIDE])
        reach = SLAB // 2
        even = cos_inverse(LENGTH, fr, list(range(reach + 1)))
        odd = sin_inverse(LENGTH, fi, list(range(1, reach + 1)))
        for x in range(SLAB):
            lag = x - reach
            if lag == 0:
                value = even[0]
            elif lag > 0:
                value = even[lag] - odd[lag]
            else:
                value = even[-lag] + odd[-lag]
            finish(x, pl.ds(at, 8), value * factor_ref[x, pl.ds(at, 8), :])

    @pl.when(step == 0)
    def _():
        def body(block, carry):
            def keep(x, at, value):
                held_ref[x, at, :] = value

            scores(block, keep)
            return carry

        lax.fori_loop(0, WIDE // 8, body, 0)

    @pl.when(step == 1)
    def _():
        def body(block, carry):
            def keep(x, at, value):
                held_ref[x, at, :] = jnp.maximum(held_ref[x, at, :], value)

            scores(block, keep)
            return carry

        lax.fori_loop(0, WIDE // 8, body, 0)
        best_ref[...] = held_ref[...].astype(BF16)


def match_call(core, orients, own, other, spec, factor, first, second, small_z, small_y):
    vmem = pl.BlockSpec(memory_space=pltpu.VMEM)
    smem = pl.BlockSpec(memory_space=pltpu.SMEM)
    cube = EDGE * EDGE
    return pl.pallas_call(
        match_kernel,
        grid=(2,),
        out_shape=jax.ShapeDtypeStruct((SLAB, WIDE, WIDE), BF16),
        in_specs=[smem, smem] + [vmem] * 8,
        out_specs=vmem,
        scratch_shapes=[
            pltpu.VMEM((cube, EDGE), F32),
            pltpu.VMEM((cube, EDGE), F32),
            pltpu.VMEM((cube, EDGE), F32),
            pltpu.VMEM((EDGE, 8, WIDE), F32),
            pltpu.VMEM((FREQS * EDGE, 2 * EDGE), F32),
            pltpu.VMEM((PAIRS, 2 * EDGE, 2 * WIDE), BF16),
            pltpu.VMEM((FREQS, WIDE, 2 * WIDE), BF16),
            pltpu.VMEM((PAIRS, 2 * WIDE, 2 * WIDE), BF16),
            pltpu.VMEM((PAIRS, 2 * WIDE, 2 * WIDE), F32),
            pltpu.VMEM((SLAB, WIDE, WIDE), F32),
        ],
        compiler_params=pltpu.CompilerParams(vmem_limit_bytes=40 << 20),
        cost_estimate=pl.CostEstimate(flops=8_000_000_000, transcendentals=0, bytes_accessed=6_000_000),
        name="match",
    )(core, orients, own, other, spec, factor, first, second, small_z, small_y)


def shifted(value, axis, by):
    length = lax.axis_size(axis)
    pairs = [(i, i + by) for i in range(length) if 0 <= i + by < length]
    return lax.ppermute(value, axis, pairs)


def swapped(value, axis):
    return lax.ppermute(value, axis, [(0, 1), (1, 0)])


def by_offset(value, axes, offset):
    sizes = [lax.axis_size(axis) for axis in axes]

    def flat(spots):
        index = 0
        for spot_at, size in zip(spots, sizes):
            index = index * size + spot_at % size
        return index

    pairs = [
        (flat(spots), flat([at + by for at, by in zip(spots, offset)]))
        for spots in itertools.product(*[range(size) for size in sizes])
    ]
    return lax.ppermute(value, axes, pairs)


def shards(tomogram, templates, owners, orient_ids, slice_mask):
    core_arg = lax.axis_index("core").astype(jnp.int32)[None]
    first, second, small_z, small_y = tables()
    rows, columns = lax.axis_size("tile_1"), lax.axis_size("tile_2")
    members = lax.axis_size("tile_0")
    root_x = lax.rem(owners[0], columns)
    root_y = lax.rem(lax.div(owners[0], columns), rows)
    root_z = lax.div(owners[0], rows * columns)
    off_y = lax.rem(lax.axis_index("tile_1") + rows - root_y, rows)
    off_x = lax.rem(lax.axis_index("tile_2") + columns - root_x, columns)
    even_y = lax.rem(off_y, 2) == 0

    slices, sent = prep_call(core_arg, tomogram, templates, members)
    near = shifted(slices, TILE, -1)
    far = shifted(slices, TILE, -2)
    got = lax.all_to_all(sent, "tile_0", 0, 0, tiled=True)
    other_id = swapped(orient_ids[0], "far")
    half = lax.dynamic_index_in_dim(got, root_z, 0, keepdims=False)
    halo = jnp.stack([near, far])
    other_halo = swapped(halo, "core")

    axes = ("tile_1", "tile_2")
    half = jnp.where(off_y == 2, by_offset(half, axes, (2, 0)), half)
    from_y = by_offset(half, axes, (1, 0))
    from_x = by_offset(half, axes, (0, 1))
    from_both = by_offset(half, axes, (1, 1))
    half = jnp.where(
        off_x == 0,
        jnp.where(even_y, half, from_y),
        jnp.where(even_y, from_x, from_both),
    )
    other_half = swapped(half, "core")

    spec = spectrum_call(core_arg, tomogram, halo, other_halo, first, second)
    factor = factor_call(core_arg, tomogram, halo, other_halo)

    orients = jnp.concatenate([orient_ids[0], other_id])
    best = match_call(
        core_arg, orients, half, other_half, spec, factor, first, second, small_z, small_y
    )
    best = jnp.maximum(best, swapped(best, "core"))
    return best.astype(F32) * slice_mask.astype(F32)[:, None, None]


def solution(mesh):
    torus = Mesh(
        mesh.devices.reshape(8, 4, 2, 2, 2), ("tile_0", "tile_1", "tile_2", "far", "core")
    )
    in_specs = (P(TILE, None, None), P(TILE, None, None, None), P(), P(None, ("far", "core")), P(TILE))
    out_specs = P(TILE, None, None)
    return jax.shard_map(
        shards, mesh=torus, in_specs=in_specs, out_specs=out_specs, check_vma=False
    )
```

profile of v0, /device:TPU:1, one launch (start us, length us, event | category | flops | bytes accessed | tf_op | source)
XLA Modules:
  0.0 63.1 jit_solution(10820054110106755410)
XLA Ops:
  0.0 0.0 copy-start
  0.0 1.9 %prep.1 = (bf16[8,128,128]{2,1,0:T(8,128)(2,1)}, bf16[8,128,128]{2,1,0:T(8,128)(2,1)}) custom-call(s32[1]{0:T(128)} %bitcast.core_ref, bf16[16,128,128]{2,1,0:T(8,128)(2,1)} %tomo_ref.5, bf16[1,32,32,32]{3,2,1,0:T(8,128)(2,1)} %temp_ref.1), custom_call_target="tpu_custom_call" | custom-call | tf_op jit(solution)/shard_map/prep/pallas_call | solution.py:282
  1.9 9.0 %all-to-all-start = ((bf16[8,128,128]{2,1,0:T(8,128)(2,1)}), bf16[8,128,128]{2,1,0:T(8,128)(2,1)S(1)}, u32[]{:S(2)}, u32[]{:S(2)}) async-start(bf16[8,128,128]{2,1,0:T(8,128)(2,1)} %get-tuple-element.7), calls=%async_computation | async-start | bytes 524288 | tf_op jit(solution)/shard_map/all_to_all | solution.py:532
  10.9 1.3 %collective-permute-start.6 = (bf16[8,128,128]{2,1,0:T(8,128)(2,1)}, bf16[8,128,128]{2,1,0:T(8,128)(2,1)S(1)}, u32[]{:S(2)}, u32[]{:S(2)}) collective-permute-start(bf16[8,128,128]{2,1,0:T(8,128)(2,1)} %get-tuple-element.8), channel_id=1, source_target_pairs={{4,0},{8,4},{12,8},{16,12},{20,16},{24,20},{28,24},{32,28},{36,32}... | collective-permute-start | bytes 786440 | tf_op jit(solution)/shard_map/ppermute | solution.py:494
  12.2 1.3 %collective-permute-start.7 = (bf16[8,128,128]{2,1,0:T(8,128)(2,1)}, bf16[8,128,128]{2,1,0:T(8,128)(2,1)S(1)}, u32[]{:S(2)}, u32[]{:S(2)}) collective-permute-start(bf16[8,128,128]{2,1,0:T(8,128)(2,1)} %get-tuple-element.8), channel_id=1, source_target_pairs={{8,0},{12,4},{16,8},{20,12},{24,16},{28,20},{32,24},{36,28},{40,32... | collective-permute-start | bytes 786440 | tf_op jit(solution)/shard_map/ppermute | solution.py:494
  13.5 2.8 %collective-permute-start = (s32[1]{0:T(128)}, s32[1]{0:T(128)}, u32[]{:S(2)}, u32[]{:S(2)}) collective-permute-start(s32[1]{0:T(128)} %bitcast.1), channel_id=1, source_target_pairs={{0,2},{2,0},{1,3},{3,1},{4,6},{6,4},{5,7},{7,5},{8,10},{10,8},{9,1... | collective-permute-start | bytes 20 | tf_op jit(solution)/shard_map/ppermute | solution.py:498
  17.6 3.7 %all-to-all-done = bf16[8,128,128]{2,1,0:T(8,128)(2,1)S(1)} async-done(((bf16[8,128,128]{2,1,0:T(8,128)(2,1)}), bf16[8,128,128]{2,1,0:T(8,128)(2,1)S(1)}, u32[]{:S(2)}, u32[]{:S(2)}) %all-to-all-start) | async-done | bytes 262176 | tf_op jit(solution)/shard_map/all_to_all | solution.py:532
  21.4 2.9 %collective-permute-start.1 = (bf16[128,128]{1,0:T(8,128)(2,1)S(1)}, bf16[128,128]{1,0:T(8,128)(2,1)S(1)}, u32[]{:S(2)}, u32[]{:S(2)}) collective-permute-start(bf16[128,128]{1,0:T(8,128)(2,1)S(1)} %dynamic-slice_bitcast_fusion), channel_id=1, source_target_pairs={{0,16},{4,20},{8,24},{12,28},{16,0},{20,4},{24,8},{28,12},{1,17},{... | collective-permute-start | bytes 98312 | tf_op jit(solution)/shard_map/ppermute | solution.py:514
  24.3 0.0 collective-permute-done.6
  24.3 0.0 collective-permute-done.7
  24.3 0.1 pad_maximum_fusion.own_ref
  24.3 2.7 %collective-permute-start.8 = (bf16[2,8,128,128]{3,2,1,0:T(8,128)(2,1)S(1)}, bf16[2,8,128,128]{3,2,1,0:T(8,128)(2,1)S(1)}, u32[]{:S(2)}, u32[]{:S(2)}) collective-permute-start(bf16[2,8,128,128]{3,2,1,0:T(8,128)(2,1)S(1)} %pad_maximum_fusion.own_ref), channel_id=1, source_target_pairs={{0,1},{1,0},{2,3},{3,2},{4,5},{5,4},{6,7},{7,6},{8,9},{9,8},{10,11... | collective-permute-start | bytes 1572872 | tf_op jit(solution)/shard_map/ppermute | solution.py:498
  27.0 0.0 collective-permute-done.1
  27.1 0.5 collective-permute-start.2
  27.5 4.5 %collective-permute-start.3 = (bf16[128,128]{1,0:T(8,128)(2,1)S(1)}, bf16[128,128]{1,0:T(8,128)(2,1)S(1)}, u32[]{:S(2)}, u32[]{:S(2)}) collective-permute-start(bf16[128,128]{1,0:T(8,128)(2,1)S(1)} %broadcast_select_fusion), channel_id=1, source_target_pairs={{0,4},{4,0},{8,12},{12,8},{16,20},{20,16},{24,28},{28,24},{1,5},{5... | collective-permute-start | bytes 98312 | tf_op jit(solution)/shard_map/ppermute | solution.py:514
  32.0 0.0 collective-permute-start.4
  32.0 0.0 collective-permute-done
  32.0 0.6 %pad_add_fusion.orient_ref = s32[2]{0:T(128)S(1)} fusion(s32[1]{0:T(128)} %collective-permute-done, s32[1]{0:T(128)} %bitcast.12), kind=kLoop, calls=%fused_computation.5 | loop fusion | flops 2 | bytes 16 | tf_op jit(solution)/shard_map/concatenate | solution.py:553
  32.7 4.5 %collective-permute-done.2 = bf16[128,128]{1,0:T(8,128)(2,1)S(1)} collective-permute-done((bf16[128,128]{1,0:T(8,128)(2,1)S(1)}, bf16[128,128]{1,0:T(8,128)(2,1)S(1)}, u32[]{:S(2)}, u32[]{:S(2)}) %collective-permute-start.2) | collective-permute-done | bytes 32800 | tf_op jit(solution)/shard_map/ppermute | solution.py:514
  37.2 0.0 collective-permute-done.3
  37.2 1.4 %collective-permute-done.4 = bf16[128,128]{1,0:T(8,128)(2,1)S(1)} collective-permute-done((bf16[128,128]{1,0:T(8,128)(2,1)S(1)}, bf16[128,128]{1,0:T(8,128)(2,1)S(1)}, u32[]{:S(2)}, u32[]{:S(2)}) %collective-permute-start.4) | collective-permute-done | bytes 32800 | tf_op jit(solution)/shard_map/ppermute | solution.py:514
  38.6 0.0 copy-start.1
  38.6 0.0 copy-start.2
  38.6 1.3 %collective-permute-start.5 = (bf16[128,128]{1,0:T(8,128)(2,1)S(1)}, bf16[128,128]{1,0:T(8,128)(2,1)S(1)}, u32[]{:S(2)}, u32[]{:S(2)}) collective-permute-start(bf16[128,128]{1,0:T(8,128)(2,1)S(1)} %select_select_fusion.own_ref), channel_id=1, source_target_pairs={{0,1},{1,0},{2,3},{3,2},{4,5},{5,4},{6,7},{7,6},{8,9},{9,8},{10,11... | collective-permute-start | bytes 98312 | tf_op jit(solution)/shard_map/ppermute | solution.py:498
  39.9 0.0 collective-permute-done.8.other_ref
  39.9 0.0 copy-done
  39.9 7.8 %factor.1.factor_ref = f32[16,128,128]{2,1,0:T(8,128)S(1)} custom-call(s32[1]{0:T(128)} %bitcast.core_ref, bf16[16,128,128]{2,1,0:T(8,128)(2,1)S(1)} %copy-done, bf16[2,8,128,128]{3,2,1,0:T(8,128)(2,1)S(1)} %pad_maximum_fusion.own_ref, bf16[2,8,128,128]{3,2,1,0:T(8,128)(2,1)S(1)} %collective-permute-done.8.other_ref), custom_call_target="tpu_custom_call" | custom-call | flops 4000000000 | bytes 6000000 | tf_op jit(solution)/shard_map/factor/pallas_call | solution.py:256
  47.7 0.0 copy-done.1
  47.7 0.0 copy-done.2
  47.7 0.0 copy-start.3
  47.7 0.0 copy-start.4
  47.8 3.4 %spectrum.1.spec_ref = bf16[13,256,256]{2,1,0:T(8,128)(2,1)S(1)} custom-call(s32[1]{0:T(128)} %bitcast.core_ref, bf16[16,128,128]{2,1,0:T(8,128)(2,1)S(1)} %copy-done, bf16[2,8,128,128]{3,2,1,0:T(8,128)(2,1)S(1)} %pad_maximum_fusion.own_ref, bf16[2,8,128,128]{3,2,1,0:T(8,128)(2,1)S(1)} %collective-permute-done.8.other_ref, bf16[256,256]{1,0:T(8,128)(2,1)S(1)} %copy-done.1, ...), custom_call_target="tpu_custom_call" | custom-call | flops 4000000000 | bytes 6000000 | tf_op jit(solution)/shard_map/spectrum/pallas_call | solution.py:238
  51.1 0.0 copy-start.5
  51.1 0.0 collective-permute-done.5.other_ref
  51.2 0.0 copy-done.3
  51.2 0.0 copy-done.4
  51.2 8.8 %match.1 = bf16[16,128,128]{2,1,0:T(8,128)(2,1)S(1)} custom-call(s32[1]{0:T(128)} %bitcast.core_ref, s32[2]{0:T(128)S(1)} %pad_add_fusion.orient_ref, bf16[128,128]{1,0:T(8,128)(2,1)S(1)} %select_select_fusion.own_ref, bf16[128,128]{1,0:T(8,128)(2,1)S(1)} %collective-permute-done.5.other_ref, bf16[13,256,256]{2,1,0:T(8,128)(2,1)S(1)} %spectrum.1.spec_ref, ...), custom_call_target="tpu_custom_call" | custom-call | flops 8000000000 | bytes 6000000 | tf_op jit(solution)/shard_map/match/pallas_call | solution.py:467
  60.0 0.1 collective-permute-start.9
  60.1 0.0 copy-done.5
  60.1 1.9 %collective-permute-done.9 = bf16[16,128,128]{2,1,0:T(8,128)(2,1)S(1)} collective-permute-done((bf16[16,128,128]{2,1,0:T(8,128)(2,1)S(1)}, bf16[16,128,128]{2,1,0:T(8,128)(2,1)S(1)}, u32[]{:S(2)}, u32[]{:S(2)}) %collective-permute-start.9) | collective-permute-done | bytes 524320 | tf_op jit(solution)/shard_map/ppermute | solution.py:498
  62.0 1.1 %convert_multiply_fusion = f32[16,128,128]{2,1,0:T(8,128)} fusion(f32[16]{0:T(128)S(1)} %convert_element_type.23, bf16[16,128,128]{2,1,0:T(8,128)(2,1)S(1)} %match.1, bf16[16,128,128]{2,1,0:T(8,128)(2,1)S(1)} %collective-permute-done.9), kind=kLoop, calls=%fused_computation | loop fusion | flops 786432 | bytes 2097216 | tf_op jit(solution)/shard_map/mul | solution.py:558
  (4 shorter events, 0.0 us)
Async XLA Ops:
  0.0 39.9 %copy-start = (bf16[16,128,128]{2,1,0:T(8,128)(2,1)S(1)}, bf16[16,128,128]{2,1,0:T(8,128)(2,1)}, u32[]{:S(2)}) copy-start(bf16[16,128,128]{2,1,0:T(8,128)(2,1)} %tomo_ref.5) | copy-start | bytes 1572868
  1.9 19.5 %all-to-all-start = ((bf16[8,128,128]{2,1,0:T(8,128)(2,1)}), bf16[8,128,128]{2,1,0:T(8,128)(2,1)S(1)}, u32[]{:S(2)}, u32[]{:S(2)}) async-start(bf16[8,128,128]{2,1,0:T(8,128)(2,1)} %get-tuple-element.7), calls=%async_computation | async-start | bytes 524288 | tf_op jit(solution)/shard_map/all_to_all | solution.py:532
  10.9 13.4 %collective-permute-start.6 = (bf16[8,128,128]{2,1,0:T(8,128)(2,1)}, bf16[8,128,128]{2,1,0:T(8,128)(2,1)S(1)}, u32[]{:S(2)}, u32[]{:S(2)}) collective-permute-start(bf16[8,128,128]{2,1,0:T(8,128)(2,1)} %get-tuple-element.8), channel_id=1, source_target_pairs={{4,0},{8,4},{12,8},{16,12},{20,16},{24,20},{28,24},{32,28},{36,32}... | collective-permute-start | bytes 786440 | tf_op jit(solution)/shard_map/ppermute | solution.py:494
  12.2 12.1 %collective-permute-start.7 = (bf16[8,128,128]{2,1,0:T(8,128)(2,1)}, bf16[8,128,128]{2,1,0:T(8,128)(2,1)S(1)}, u32[]{:S(2)}, u32[]{:S(2)}) collective-permute-start(bf16[8,128,128]{2,1,0:T(8,128)(2,1)} %get-tuple-element.8), channel_id=1, source_target_pairs={{8,0},{12,4},{16,8},{20,12},{24,16},{28,20},{32,24},{36,28},{40,32... | collective-permute-start | bytes 786440 | tf_op jit(solution)/shard_map/ppermute | solution.py:494
  13.5 18.6 %collective-permute-start = (s32[1]{0:T(128)}, s32[1]{0:T(128)}, u32[]{:S(2)}, u32[]{:S(2)}) collective-permute-start(s32[1]{0:T(128)} %bitcast.1), channel_id=1, source_target_pairs={{0,2},{2,0},{1,3},{3,1},{4,6},{6,4},{5,7},{7,5},{8,10},{10,8},{9,1... | collective-permute-start | bytes 20 | tf_op jit(solution)/shard_map/ppermute | solution.py:498
  21.4 5.7 %collective-permute-start.1 = (bf16[128,128]{1,0:T(8,128)(2,1)S(1)}, bf16[128,128]{1,0:T(8,128)(2,1)S(1)}, u32[]{:S(2)}, u32[]{:S(2)}) collective-permute-start(bf16[128,128]{1,0:T(8,128)(2,1)S(1)} %dynamic-slice_bitcast_fusion), channel_id=1, source_target_pairs={{0,16},{4,20},{8,24},{12,28},{16,0},{20,4},{24,8},{28,12},{1,17},{... | collective-permute-start | bytes 98312 | tf_op jit(solution)/shard_map/ppermute | solution.py:514
  24.3 15.5 %collective-permute-start.8 = (bf16[2,8,128,128]{3,2,1,0:T(8,128)(2,1)S(1)}, bf16[2,8,128,128]{3,2,1,0:T(8,128)(2,1)S(1)}, u32[]{:S(2)}, u32[]{:S(2)}) collective-permute-start(bf16[2,8,128,128]{3,2,1,0:T(8,128)(2,1)S(1)} %pad_maximum_fusion.own_ref), channel_id=1, source_target_pairs={{0,1},{1,0},{2,3},{3,2},{4,5},{5,4},{6,7},{7,6},{8,9},{9,8},{10,11... | collective-permute-start | bytes 1572872 | tf_op jit(solution)/shard_map/ppermute | solution.py:498
  27.1 10.1 %collective-permute-start.2 = (bf16[128,128]{1,0:T(8,128)(2,1)S(1)}, bf16[128,128]{1,0:T(8,128)(2,1)S(1)}, u32[]{:S(2)}, u32[]{:S(2)}) collective-permute-start(bf16[128,128]{1,0:T(8,128)(2,1)S(1)} %broadcast_select_fusion), channel_id=1, source_target_pairs={{0,8},{4,12},{8,16},{12,20},{16,24},{20,28},{24,0},{28,4},{1,9},{5... | collective-permute-start | bytes 98312 | tf_op jit(solution)/shard_map/ppermute | solution.py:514
  27.5 9.6 %collective-permute-start.3 = (bf16[128,128]{1,0:T(8,128)(2,1)S(1)}, bf16[128,128]{1,0:T(8,128)(2,1)S(1)}, u32[]{:S(2)}, u32[]{:S(2)}) collective-permute-start(bf16[128,128]{1,0:T(8,128)(2,1)S(1)} %broadcast_select_fusion), channel_id=1, source_target_pairs={{0,4},{4,0},{8,12},{12,8},{16,20},{20,16},{24,28},{28,24},{1,5},{5... | collective-permute-start | bytes 98312 | tf_op jit(solution)/shard_map/ppermute | solution.py:514
  32.0 6.6 %collective-permute-start.4 = (bf16[128,128]{1,0:T(8,128)(2,1)S(1)}, bf16[128,128]{1,0:T(8,128)(2,1)S(1)}, u32[]{:S(2)}, u32[]{:S(2)}) collective-permute-start(bf16[128,128]{1,0:T(8,128)(2,1)S(1)} %broadcast_select_fusion), channel_id=1, source_target_pairs={{0,12},{4,8},{8,20},{12,16},{16,28},{20,24},{24,4},{28,0},{1,13},{... | collective-permute-start | bytes 98312 | tf_op jit(solution)/shard_map/ppermute | solution.py:514
  38.6 9.1 %copy-start.1 = (bf16[256,256]{1,0:T(8,128)(2,1)S(1)}, bf16[256,256]{1,0:T(8,128)(2,1)}, u32[]{:S(2)}) copy-start(bf16[256,256]{1,0:T(8,128)(2,1)} %constant.56.first_ref) | copy-start | bytes 393220
  38.6 9.1 %copy-start.2 = (bf16[256,256]{1,0:T(8,128)(2,1)S(1)}, bf16[256,256]{1,0:T(8,128)(2,1)}, u32[]{:S(2)}) copy-start(bf16[256,256]{1,0:T(8,128)(2,1)} %constant.57.second_ref) | copy-start | bytes 393220
  38.6 12.5 %collective-permute-start.5 = (bf16[128,128]{1,0:T(8,128)(2,1)S(1)}, bf16[128,128]{1,0:T(8,128)(2,1)S(1)}, u32[]{:S(2)}, u32[]{:S(2)}) collective-permute-start(bf16[128,128]{1,0:T(8,128)(2,1)S(1)} %select_select_fusion.own_ref), channel_id=1, source_target_pairs={{0,1},{1,0},{2,3},{3,2},{4,5},{5,4},{6,7},{7,6},{8,9},{9,8},{10,11... | collective-permute-start | bytes 98312 | tf_op jit(solution)/shard_map/ppermute | solution.py:498
  47.7 3.4 %copy-start.3 = (bf16[2,256,64]{2,1,0:T(8,128)(2,1)S(1)}, bf16[2,256,64]{2,1,0:T(8,128)(2,1)}, u32[]{:S(2)}) copy-start(bf16[2,256,64]{2,1,0:T(8,128)(2,1)} %constant.59.small_y_ref) | copy-start | bytes 196612
  47.7 3.4 %copy-start.4 = (bf16[2,64,256]{2,1,0:T(8,128)(2,1)S(1)}, bf16[2,64,256]{2,1,0:T(8,128)(2,1)}, u32[]{:S(2)}) copy-start(bf16[2,64,256]{2,1,0:T(8,128)(2,1)} %constant.58.small_z_ref) | copy-start | bytes 196612
  51.1 8.9 %copy-start.5 = (s32[16]{0:T(128)S(1)}, s32[16]{0:T(128)}, u32[]{:S(2)}) copy-start(s32[16]{0:T(128)} %param.13) | copy-start | bytes 196
  60.0 2.0 %collective-permute-start.9 = (bf16[16,128,128]{2,1,0:T(8,128)(2,1)S(1)}, bf16[16,128,128]{2,1,0:T(8,128)(2,1)S(1)}, u32[]{:S(2)}, u32[]{:S(2)}) collective-permute-start(bf16[16,128,128]{2,1,0:T(8,128)(2,1)S(1)} %match.1), channel_id=1, source_target_pairs={{0,1},{1,0},{2,3},{3,2},{4,5},{5,4},{6,7},{7,6},{8,9},{9,8},{10,11... | collective-permute-start | bytes 1572872 | tf_op jit(solution)/shard_map/ppermute | solution.py:498
where the time goes:
time: 63.4 us; the launch traced here: 63.1 us
  starting transfers between devices  26.4 us (42%)
  Pallas kernels  21.8 us (34%)
  waiting for transfers between devices  11.5 us (18%)
  other arithmetic  1.84 us (3%)
  between operations  1.51 us (2%)
    all_to_all x1, starting transfers between devices, shards(): got = lax.all_to_all(sent, 'tile_0', 0, 0, tiled=True)  9 us
    pallas_call x1, Pallas kernels, match_call(): pl.pallas_call(match_kernel, grid=(2,), out_shape=jax.ShapeDtypeStruct((S...  8.78 us
    ppermute x4, starting transfers between devices, by_offset(): return lax.ppermute(value, axes, pairs)  7.9 us
    pallas_call x1, Pallas kernels, factor_call(): pl.pallas_call(factor_kernel, out_shape=jax.ShapeDtypeStruct((SLAB, WIDE,...  7.81 us
    ppermute x4, starting transfers between devices, swapped(): return lax.ppermute(value, axis, [(0, 1), (1, 0)])  6.9 us
    ppermute x4, waiting for transfers between devices, by_offset(): return lax.ppermute(value, axes, pairs)  5.9 us
    all_to_all x1, waiting for transfers between devices, shards(): got = lax.all_to_all(sent, 'tile_0', 0, 0, tiled=True)  3.73 us
    pallas_call x1, Pallas kernels, spectrum_call(): pl.pallas_call(spectrum_kernel, out_shape=jax.ShapeDtypeStruct((PAIRS, 2...  3.37 us
  transfers between devices with their start and end apart: 11, of which 4 were waited for; matrix products, arithmetic and copies ran while one was open for 1% of the time, Pallas kernels for 18%

commit v1 on v0

v1 whole, which is shorter than its diff:
```python
import itertools
import math

import jax
import jax.numpy as jnp
import numpy as np
from jax import lax
from jax.experimental import pallas as pl
from jax.experimental.pallas import tpu as pltpu
from jax.sharding import Mesh
from jax.sharding import PartitionSpec as P


TILE = ("tile_0", "tile_1", "tile_2")
EDGE = 32
TAIL = 16
SLAB = 16
WIDE = 128
LENGTH = 48
HALF = LENGTH // 2
FREQS = HALF + 1
PAIRS = (FREQS + 1) // 2
BF16 = jnp.bfloat16
F32 = jnp.float32


def plus(a, b):
    if a is None:
        return b
    return a if b is None else a + b


def minus(a, b):
    if b is None:
        return a
    return -b if a is None else a - b


def weighted(terms):
    total = None
    for value, weight in terms:
        if value is None or abs(weight) < 1e-9:
            continue
        if abs(abs(weight) - 1.0) < 1e-9:
            part = value
        else:
            part = value * jnp.float32(abs(weight))
        if weight > 0:
            total = plus(total, part)
        else:
            total = minus(total, part)
    return total


def cosine(j, k, n):
    return math.cos(2.0 * math.pi * ((j * k) % n) / n)


def sine(j, k, n):
    return math.sin(2.0 * math.pi * ((j * k) % n) / n)


def cos_forward(n, e):
    half = n // 2
    if n % 4:
        return [weighted([(e[j], cosine(j, k, n)) for j in range(half + 1)]) for k in range(half + 1)]
    even = cos_forward(half, e[0::2])
    out = [None] * (half + 1)
    for k in range(n // 4 + 1):
        odd = weighted([(e[j], cosine(j, k, n)) for j in range(1, half, 2)])
        out[k] = plus(even[k], odd)
        if k < n // 4:
            out[half - k] = minus(even[k], odd)
    return out


def sin_forward(n, o):
    half = n // 2
    if n % 4:
        return [weighted([(o[j], sine(j, k, n)) for j in range(1, half)]) if k % half else None for k in range(half + 1)]
    even = sin_forward(half, o[0::2])
    out = [None] * (half + 1)
    for k in range(1, n // 4 + 1):
        odd = weighted([(o[j], sine(j, k, n)) for j in range(1, half, 2)])
        out[k] = plus(even[k], odd) if k < n // 4 else odd
        if k < n // 4:
            out[half - k] = minus(odd, even[k])
    return out


def cos_inverse(n, f, wanted):
    half, quarter = n // 2, n // 4
    if n % 4:
        return {x: weighted([(f[k], cosine(k, x, n)) for k in range(half + 1)]) for x in wanted}
    out = {}
    evens = [x // 2 for x in wanted if x % 2 == 0]
    odds = [x for x in wanted if x % 2]
    if odds:
        q = [minus(f[k], f[half - k]) for k in range(quarter)]
        for x in odds:
            out[x] = weighted([(q[k], cosine(k, x, n)) for k in range(quarter)])
    if evens:
        p = [plus(f[k], f[half - k]) for k in range(quarter)] + [f[quarter]]
        for x, value in cos_inverse(half, p, evens).items():
            out[2 * x] = value
    return out


def sin_inverse(n, g, wanted):
    half, quarter = n // 2, n // 4
    if n % 4:
        return {x: weighted([(g[k], sine(k, x, n)) for k in range(1, half)]) for x in wanted}
    out = {}
    evens = [x // 2 for x in wanted if x % 2 == 0]
    odds = [x for x in wanted if x % 2]
    if odds:
        t = [None] + [plus(g[k], g[half - k]) for k in range(1, quarter)] + [g[quarter]]
        for x in odds:
            out[x] = weighted([(t[k], sine(k, x, n)) for k in range(1, quarter + 1)])
    if evens:
        r = [None] + [minus(g[k], g[half - k]) for k in range(1, quarter)] + [None]
        for x, value in sin_inverse(half, r, evens).items():
            out[2 * x] = value
    return out


def slices_forward(s):
    e = [s[0]] + [plus(s[j], s[LENGTH - j]) for j in range(1, HALF)] + [s[HALF]]
    o = [None] + [minus(s[j], s[LENGTH - j]) for j in range(1, HALF)] + [None]
    return cos_forward(LENGTH, e), sin_forward(LENGTH, o)


def tables():
    def table(rows, cols):
        angle = (np.outer(np.arange(rows), np.arange(cols)) % WIDE).astype(np.float32)
        angle = angle * np.float32(2.0 * math.pi / WIDE)
        return np.cos(angle), np.sin(angle)

    c, s = table(WIDE, WIDE)
    first = np.block([[c, -s], [s, c]])
    second = np.block([[c, s], [-s, c]])
    small_z, small_y = [], []
    for flip in (False, True):
        c, s = table(EDGE, WIDE)
        if flip:
            c, s = c[::-1], s[::-1]
        small_z.append(np.block([[c, -s], [s, c]]))
        small_y.append(np.block([[c.T, s.T], [-s.T, c.T]]))
    behind = (np.arange(WIDE)[:, None] - np.arange(WIDE)[None, :]) % WIDE
    band = np.concatenate([behind < EDGE] * 3)
    return [
        jnp.asarray(t.astype(np.float32)).astype(BF16)
        for t in (first, second, np.stack(small_z), np.stack(small_y), band)
    ]


def dot(a, b):
    return jnp.dot(a, b, preferred_element_type=F32)


def spot(k):
    return k // 2, (k % 2) * WIDE


def fill_halo(core_ref, own_ref, other_ref, halo_ref):
    core = core_ref[0]
    for hop in range(2):
        halo_ref[pl.ds(hop * SLAB + 8 * core, 8)] = own_ref[hop]
        halo_ref[pl.ds(hop * SLAB + 8 * (1 - core), 8)] = other_ref[hop]


def load_rows(tomo_ref, halo_ref, at):
    s = [tomo_ref[j, at, :] if j < SLAB else halo_ref[j - SLAB, at, :] for j in range(LENGTH - 1)]
    return [value.astype(F32) for value in s]


def spectrum_kernel(core_ref, tomo_ref, own_ref, other_ref, first_ref, second_ref, spec_ref,
                    halo_ref, x_ref, z_ref):
    fill_halo(core_ref, own_ref, other_ref, halo_ref)

    def rows(step, carry):
        at = pl.ds(pl.multiple_of(step * 16, 16), 16)
        real, imag = slices_forward(load_rows(tomo_ref, halo_ref, at) + [None])
        for k in range(FREQS):
            x_ref[k, at, :WIDE] = real[k].astype(BF16)
            if imag[k] is None:
                x_ref[k, at, WIDE:] = jnp.zeros((16, WIDE), BF16)
            else:
                x_ref[k, at, WIDE:] = (-imag[k]).astype(BF16)
        return carry

    lax.fori_loop(0, WIDE // 16, rows, 0)

    for k in range(FREQS):
        pair, lane = spot(k)
        moved = dot(x_ref[k], first_ref[...]).astype(BF16)
        z_ref[pair, :WIDE, lane:lane + WIDE] = moved[:, :WIDE]
        z_ref[pair, WIDE:, lane:lane + WIDE] = moved[:, WIDE:]
    for pair in range(PAIRS):
        width = WIDE if pair == PAIRS - 1 else 2 * WIDE
        spec_ref[pair, :, :width] = dot(second_ref[...], z_ref[pair, :, :width]).astype(BF16)
        if width == WIDE:
            spec_ref[pair, :, WIDE:] = jnp.zeros((2 * WIDE, WIDE), BF16)


def split(value):
    high = value.astype(BF16)
    rest = value - high.astype(F32)
    middle = rest.astype(BF16)
    return high, middle, (rest - middle.astype(F32)).astype(BF16)


def factor_kernel(core_ref, tomo_ref, own_ref, other_ref, band_ref, factor_ref, halo_ref, sum_ref, square_ref):
    fill_halo(core_ref, own_ref, other_ref, halo_ref)

    def windows(step, carry):
        at = pl.ds(pl.multiple_of(step * 16, 16), 16)
        s = load_rows(tomo_ref, halo_ref, at)
        for target, field in ((sum_ref, s), (square_ref, [value * value for value in s])):
            for reach in (1, 2, 4, 8, 16):
                field = [field[j] + field[j + reach] for j in range(len(field) - reach)]
            for x in range(SLAB):
                target[x, at, :] = field[x]
        return carry

    lax.fori_loop(0, WIDE // 16, windows, 0)

    volume = float(EDGE**3)

    def along_y(field):
        for reach in (1, 2, 4, 8, 16):
            field = field + pltpu.roll(field, WIDE - reach, 0)
        return jnp.concatenate(split(field), axis=1)

    def scale(x, carry):
        both = jnp.concatenate([along_y(sum_ref[x]), along_y(square_ref[x])], axis=0)
        box = dot(both, band_ref[...]) / volume
        mean_t, mean_sq = box[:WIDE], box[WIDE:]
        root = lax.rsqrt(mean_sq - mean_t * mean_t + 1e-05) / jnp.float32(math.sqrt(volume))
        factor_ref[x] = root * jnp.float32(2.0 / (LENGTH * WIDE * WIDE))
        return carry

    lax.fori_loop(0, SLAB, scale, 0, unroll=4)


def spectrum_call(core, tomogram, own, other, first, second):
    vmem = pl.BlockSpec(memory_space=pltpu.VMEM)
    return pl.pallas_call(
        spectrum_kernel,
        out_shape=jax.ShapeDtypeStruct((PAIRS, 2 * WIDE, 2 * WIDE), BF16),
        in_specs=[pl.BlockSpec(memory_space=pltpu.SMEM)] + [vmem] * 5,
        out_specs=vmem,
        scratch_shapes=[
            pltpu.VMEM((2 * SLAB, WIDE, WIDE), BF16),
            pltpu.VMEM((FREQS, WIDE, 2 * WIDE), BF16),
            pltpu.VMEM((PAIRS, 2 * WIDE, 2 * WIDE), BF16),
        ],
        compiler_params=pltpu.CompilerParams(vmem_limit_bytes=40 << 20),
        cost_estimate=pl.CostEstimate(flops=4_000_000_000, transcendentals=0, bytes_accessed=6_000_000),
        name="spectrum",
    )(core, tomogram, own, other, first, second)


def factor_call(core, tomogram, own, other, band):
    vmem = pl.BlockSpec(memory_space=pltpu.VMEM)
    return pl.pallas_call(
        factor_kernel,
        out_shape=jax.ShapeDtypeStruct((SLAB, WIDE, WIDE), F32),
        in_specs=[pl.BlockSpec(memory_space=pltpu.SMEM)] + [vmem] * 4,
        out_specs=vmem,
        scratch_shapes=[
            pltpu.VMEM((2 * SLAB, WIDE, WIDE), BF16),
            pltpu.VMEM((SLAB, WIDE, WIDE), F32),
            pltpu.VMEM((SLAB, WIDE, WIDE), F32),
        ],
        compiler_params=pltpu.CompilerParams(vmem_limit_bytes=40 << 20),
        cost_estimate=pl.CostEstimate(flops=4_000_000_000, transcendentals=0, bytes_accessed=6_000_000),
        name="factor",
    )(core, tomogram, own, other, band)


def prep_kernel(core_ref, orient_ref, temp_ref, packed_ref):
    values = temp_ref[0].astype(F32).reshape(SLAB * EDGE, EDGE)
    rows = 4 * EDGE
    packed = jnp.concatenate([values[g * rows:(g + 1) * rows] for g in range(4)], axis=1).astype(BF16)
    index = jnp.full((TAIL, WIDE), orient_ref[0], jnp.int32).astype(F32).astype(BF16)
    for member in range(packed_ref.shape[0]):
        packed_ref[member, :WIDE] = packed
        packed_ref[member, WIDE:] = index


def prep_call(core, orient, templates, members):
    return pl.pallas_call(
        prep_kernel,
        out_shape=jax.ShapeDtypeStruct((members, WIDE + TAIL, WIDE), BF16),
        grid_spec=pltpu.PrefetchScalarGridSpec(
            num_scalar_prefetch=2,
            grid=(1,),
            in_specs=[
                pl.BlockSpec((1, EDGE // 2, EDGE, EDGE), lambda i, core, orient: (0, core[0], 0, 0)),
            ],
            out_specs=pl.BlockSpec((members, WIDE + TAIL, WIDE), lambda i, core, orient: (0, 0, 0)),
        ),
        name="prep",
    )(core, orient, templates)


def match_kernel(core_ref, orient_ref, across_ref, own_ref, other_ref, spec_ref, factor_ref, first_ref, second_ref,
                 small_z_ref, small_y_ref, best_ref,
                 base_ref, cube_ref, cube_out_ref, packed_ref, a_ref, z_ref, p_ref, q_ref, f_ref, held_ref):
    core = core_ref[0]
    for mine, half_ref in ((core, own_ref), (1 - core, other_ref)):
        values = half_ref[:WIDE].astype(F32)
        for group in range(4):
            start = pl.multiple_of((16 * mine + 4 * group) * EDGE, 128)
            base_ref[pl.ds(start, 4 * EDGE), :] = values[:, group * EDGE:(group + 1) * EDGE]
    values = base_ref[...]
    total = float(EDGE**3)
    center = jnp.sum(values) / total
    values = values - center
    spread = jnp.sum(values * values) / total
    base_ref[...] = (values * lax.rsqrt(spread + 1e-05)).astype(BF16).astype(F32)

    across = jnp.max(across_ref[WIDE:].astype(F32)).astype(jnp.int32)

    def orientation(step, carry):
        index = jnp.where(step == 0, orient_ref[0], across)
        order = index // 4
        flips = index % 4
        odd_order = order >= 3
        turn_a = (order == 2) | (order == 3) | (order == 4)
        turn_b = (order == 1) | (order == 2) | (order == 4) | (order == 5)
        turn_c = (order == 1) | (order == 4)
        flip_y = flips % 2
        flip_z = flips // 2
        middle = ((flips == 1) | (flips == 2)).astype(jnp.int32)
        flip_x = jnp.where(odd_order, 1 - middle, middle)

        def swap_last(source, target):
            for a in range(EDGE):
                at = slice(a * EDGE, (a + 1) * EDGE)
                target[at, :] = source[at, :].T

        def copy(source, target):
            target[...] = source[...]

        @pl.when(turn_a)
        def _():
            swap_last(base_ref, cube_ref)

        @pl.when(jnp.logical_not(turn_a))
        def _():
            copy(base_ref, cube_ref)

        @pl.when(turn_b)
        def _():
            for b in range(EDGE):
                cube_out_ref[b * EDGE:(b + 1) * EDGE, :] = cube_ref[pl.ds(b, EDGE, stride=EDGE), :]

        @pl.when(jnp.logical_not(turn_b))
        def _():
            copy(cube_ref, cube_out_ref)

        @pl.when(turn_c)
        def _():
            swap_last(cube_out_ref, cube_ref)

        @pl.when(jnp.logical_not(turn_c))
        def _():
            copy(cube_out_ref, cube_ref)

        for x in range(EDGE):
            tile = cube_ref[x * EDGE:(x + 1) * EDGE, :]
            packed_ref[x] = jnp.concatenate([tile[8 * g:8 * g + 8] for g in range(4)], axis=1)

        s = [None] * LENGTH
        for i in range(EDGE):
            s[i + SLAB // 2] = packed_ref[jnp.where(flip_x == 1, EDGE - 1 - i, i)]
        real, imag = slices_forward(s)
        for k in range(FREQS):
            share = 0.5 if k in (0, HALF) else 1.0
            for g in range(4):
                at = slice(k * EDGE + 8 * g, k * EDGE + 8 * g + 8)
                lanes = slice(g * EDGE, (g + 1) * EDGE)
                a_ref[at, :EDGE] = real[k][:, lanes] * jnp.float32(share)
                if imag[k] is None:
                    a_ref[at, EDGE:2 * EDGE] = jnp.zeros((8, EDGE), F32)
                else:
                    a_ref[at, EDGE:2 * EDGE] = -imag[k][:, lanes]

        moved = dot(a_ref[...].astype(BF16), small_z_ref[flip_z]).astype(BF16)
        for k in range(FREQS):
            pair, lane = spot(k)
            part = moved[k * EDGE:(k + 1) * EDGE]
            z_ref[pair, :EDGE, lane:lane + WIDE] = part[:, :WIDE]
            z_ref[pair, EDGE:, lane:lane + WIDE] = part[:, WIDE:]

        small_y = small_y_ref[flip_y]
        for pair in range(PAIRS):
            width = WIDE if pair == PAIRS - 1 else 2 * WIDE
            temp = dot(small_y, z_ref[pair, :, :width])
            slab = spec_ref[pair, :, :width].astype(F32)
            temp_r, temp_i = temp[:WIDE], temp[WIDE:]
            slab_r, slab_i = slab[:WIDE], slab[WIDE:]
            prod_r = (slab_r * temp_r + slab_i * temp_i).astype(BF16)
            prod_i = (slab_i * temp_r - slab_r * temp_i).astype(BF16)
            for part in range(width // WIDE):
                k = 2 * pair + part
                lanes = slice(part * WIDE, (part + 1) * WIDE)
                p_ref[k, :, :WIDE] = prod_r[:, lanes]
                p_ref[k, :, WIDE:] = prod_i[:, lanes]

        for k in range(FREQS):
            pair, lane = spot(k)
            moved = dot(p_ref[k], second_ref[...]).astype(BF16)
            q_ref[pair, :WIDE, lane:lane + WIDE] = moved[:, :WIDE]
            q_ref[pair, WIDE:, lane:lane + WIDE] = moved[:, WIDE:]
        for pair in range(PAIRS):
            width = WIDE if pair == PAIRS - 1 else 2 * WIDE
            f_ref[pair, :, :width] = dot(first_ref[...], q_ref[pair, :, :width])

        def scores(block, finish):
            at = pl.multiple_of(block * 8, 8)
            fr, fi = [], []
            for k in range(FREQS):
                pair, lane = spot(k)
                fr.append(f_ref[pair, pl.ds(at, 8), lane:lane + WIDE])
                fi.append(f_ref[pair, pl.ds(WIDE + at, 8), lane:lane + WIDE])
            reach = SLAB // 2
            even = cos_inverse(LENGTH, fr, list(range(reach + 1)))
            odd = sin_inverse(LENGTH, fi, list(range(1, reach + 1)))
            for x in range(SLAB):
                lag = x - reach
                if lag == 0:
                    value = even[0]
                elif lag > 0:
                    value = even[lag] - odd[lag]
                else:
                    value = even[-lag] + odd[-lag]
                finish(x, pl.ds(at, 8), value * factor_ref[x, pl.ds(at, 8), :])

        @pl.when(step == 0)
        def _():
            def body(block, carry):
                def keep(x, at, value):
                    held_ref[x, at, :] = value

                scores(block, keep)
                return carry

            lax.fori_loop(0, WIDE // 8, body, 0)

        @pl.when(step == 1)
        def _():
            def body(block, carry):
                def keep(x, at, value):
                    held_ref[x, at, :] = jnp.maximum(held_ref[x, at, :], value)

                scores(block, keep)
                return carry

            lax.fori_loop(0, WIDE // 8, body, 0)

        return carry

    lax.fori_loop(0, 2, orientation, 0)
    best_ref[...] = held_ref[...].astype(BF16)


def match_call(core, orient, across, own, other, spec, factor, first, second, small_z, small_y):
    vmem = pl.BlockSpec(memory_space=pltpu.VMEM)
    smem = pl.BlockSpec(memory_space=pltpu.SMEM)
    cube = EDGE * EDGE
    return pl.pallas_call(
        match_kernel,
        out_shape=jax.ShapeDtypeStruct((SLAB, WIDE, WIDE), BF16),
        in_specs=[smem, smem] + [vmem] * 9,
        out_specs=vmem,
        scratch_shapes=[
            pltpu.VMEM((cube, EDGE), F32),
            pltpu.VMEM((cube, EDGE), F32),
            pltpu.VMEM((cube, EDGE), F32),
            pltpu.VMEM((EDGE, 8, WIDE), F32),
            pltpu.VMEM((FREQS * EDGE, 2 * EDGE), F32),
            pltpu.VMEM((PAIRS, 2 * EDGE, 2 * WIDE), BF16),
            pltpu.VMEM((FREQS, WIDE, 2 * WIDE), BF16),
            pltpu.VMEM((PAIRS, 2 * WIDE, 2 * WIDE), BF16),
            pltpu.VMEM((PAIRS, 2 * WIDE, 2 * WIDE), F32),
            pltpu.VMEM((SLAB, WIDE, WIDE), F32),
        ],
        compiler_params=pltpu.CompilerParams(vmem_limit_bytes=40 << 20),
        cost_estimate=pl.CostEstimate(flops=8_000_000_000, transcendentals=0, bytes_accessed=6_000_000),
        name="match",
    )(core, orient, across, own, other, spec, factor, first, second, small_z, small_y)


def shifted(value, axis, by):
    length = lax.axis_size(axis)
    pairs = [(i, i + by) for i in range(length) if 0 <= i + by < length]
    return lax.ppermute(value, axis, pairs)


def swapped(value, axis):
    return lax.ppermute(value, axis, [(0, 1), (1, 0)])


def by_offset(value, axes, offset):
    sizes = [lax.axis_size(axis) for axis in axes]

    def flat(spots):
        index = 0
        for spot_at, size in zip(spots, sizes):
            index = index * size + spot_at % size
        return index

    pairs = [
        (flat(spots), flat([at + by for at, by in zip(spots, offset)]))
        for spots in itertools.product(*[range(size) for size in sizes])
    ]
    return lax.ppermute(value, axes, pairs)


def shards(tomogram, templates, owners, orient_ids, slice_mask):
    core_arg = lax.axis_index("core").astype(jnp.int32)[None]
    first, second, small_z, small_y, band = tables()
    rows, columns = lax.axis_size("tile_1"), lax.axis_size("tile_2")
    members = lax.axis_size("tile_0")
    root_x = lax.rem(owners[0], columns)
    root_y = lax.rem(lax.div(owners[0], columns), rows)
    root_z = lax.div(owners[0], rows * columns)
    off_y = lax.rem(lax.axis_index("tile_1") + rows - root_y, rows)
    off_x = lax.rem(lax.axis_index("tile_2") + columns - root_x, columns)
    even_y = lax.rem(off_y, 2) == 0

    sent = prep_call(core_arg, orient_ids[0], templates, members)
    got = lax.all_to_all(sent, "tile_0", 0, 0, tiled=True)
    half = lax.dynamic_index_in_dim(got, root_z, 0, keepdims=False)

    slices = lax.dynamic_slice_in_dim(tomogram, SLAB // 2 * lax.axis_index("core"), SLAB // 2, 0)
    near = shifted(slices, TILE, -1)
    far = shifted(slices, TILE, -2)
    halo = jnp.stack([near, far])
    other_halo = swapped(halo, "core")

    axes = ("tile_1", "tile_2", "far")
    half = jnp.where(off_y == 2, by_offset(half, axes, (2, 0, 0)), half)
    from_y = by_offset(half, axes, (1, 0, 0))
    from_x = by_offset(half, axes, (0, 1, 1))
    from_both = by_offset(half, axes, (1, 1, 1))
    half = jnp.where(
        off_x == 0, jnp.where(even_y, half, from_y), jnp.where(even_y, from_x, from_both)
    )
    other_half = swapped(half, "core")

    factor = factor_call(core_arg, tomogram, halo, other_halo, band)
    spec = spectrum_call(core_arg, tomogram, halo, other_halo, first, second)

    best = match_call(core_arg, orient_ids[0], from_x, half, other_half, spec, factor, first, second, small_z, small_y)
    best = jnp.maximum(best, swapped(best, "core"))
    return best.astype(F32) * slice_mask.astype(F32)[:, None, None]


def solution(mesh):
    torus = Mesh(
        mesh.devices.reshape(8, 4, 2, 2, 2), ("tile_0", "tile_1", "tile_2", "far", "core")
    )
    in_specs = (P(TILE, None, None), P(TILE, None, None, None), P(), P(None, ("far", "core")), P(TILE))
    out_specs = P(TILE, None, None)
    return jax.shard_map(
        shards, mesh=torus, in_specs=in_specs, out_specs=out_specs, check_vma=False
    )
```

time: 63.4 us -> 61.7 us (0.973)
  Pallas kernels: 21.8 us -> 16.7 us
  waiting for transfers between devices: 11.5 us -> 15.3 us
  local copies, waits for them, and re-layouts: 0.04 us -> 1.01 us
  starting transfers between devices: 26.4 us -> 25.6 us
    pallas_call x1, Pallas kernels: 7.81 us -> 3.21 us  [factor_call(): pl.pallas_call(factor_kernel, out_shape=jax.ShapeDtypeStruct((SLAB, WIDE,...]
    all_to_all x1, waiting for transfers between devices: 3.73 us -> 7.03 us  [shards(): got = lax.all_to_all(sent, 'tile_0', 0, 0, tiled=True)]
    ppermute x4 -> x3, starting transfers between devices: 6.9 us -> 4.7 us  [swapped(): return lax.ppermute(value, axis, [(0, 1), (1, 0)])]
    ppermute x4, starting transfers between devices: 7.9 us -> 9.33 us  [by_offset(): return lax.ppermute(value, axes, pairs)]
    dynamic_slice x0 -> x1, local copies, waits for them, and re-layouts: none -> 0.97 us  [shards(): lax.dynamic_slice_in_dim(tomogram, SLAB // 2 * lax.axis_index('core'), SL...]
    ppermute x4 -> x3, waiting for transfers between devices: 1.88 us -> 1.88 us  [swapped(): return lax.ppermute(value, axis, [(0, 1), (1, 0)])]
  transfers between devices with their start and end apart: 11 -> 10, of which waited for: 4 -> 4; matrix products, arithmetic and copies ran while one was open for 1% -> 2% of each run, Pallas kernels for 18% -> 11%
where the time goes in v1:
time: 61.7 us; the launch traced here: 61.4 us
  starting transfers between devices  25.6 us (41%)
  Pallas kernels  16.7 us (27%)
  waiting for transfers between devices  15.3 us (25%)
  between operations  1.54 us (2%)
  other arithmetic  1.21 us (2%)
  local copies, waits for them, and re-layouts  1.01 us (2%)
    ppermute x4, starting transfers between devices, by_offset(): return lax.ppermute(value, axes, pairs)  9.33 us
    all_to_all x1, starting transfers between devices, shards(): got = lax.all_to_all(sent, 'tile_0', 0, 0, tiled=True)  9 us
    pallas_call x1, Pallas kernels, match_call(): pl.pallas_call(match_kernel, out_shape=jax.ShapeDtypeStruct((SLAB, WIDE,...  8.39 us
    all_to_all x1, waiting for transfers between devices, shards(): got = lax.all_to_all(sent, 'tile_0', 0, 0, tiled=True)  7.03 us
    ppermute x4, waiting for transfers between devices, by_offset(): return lax.ppermute(value, axes, pairs)  6.43 us
    ppermute x3, starting transfers between devices, swapped(): return lax.ppermute(value, axis, [(0, 1), (1, 0)])  4.7 us
    pallas_call x1, Pallas kernels, spectrum_call(): pl.pallas_call(spectrum_kernel, out_shape=jax.ShapeDtypeStruct((PAIRS, 2...  3.38 us
    pallas_call x1, Pallas kernels, factor_call(): pl.pallas_call(factor_kernel, out_shape=jax.ShapeDtypeStruct((SLAB, WIDE,...  3.21 us
  transfers between devices with their start and end apart: 10, of which 4 were waited for; matrix products, arithmetic and copies ran while one was open for 2% of the time, Pallas kernels for 11%

profile of v1, /device:TPU:1, one launch (start us, length us, event | category | flops | bytes accessed | tf_op | source)
XLA Modules:
  0.0 61.4 jit_solution(15586934101229793569)
XLA Ops:
  0.0 0.0 copy-start.4
  0.0 0.0 copy-start
  0.7 1.7 %prep.1 = bf16[8,144,128]{2,1,0:T(8,128)(2,1)} custom-call(s32[1]{0:T(128)} %bitcast.core_ref, s32[1]{0:T(128)} %bitcast.12.orient_ref, bf16[1,32,32,32]{3,2,1,0:T(8,128)(2,1)} %temp_ref.1), custom_call_target="tpu_custom_call" | custom-call | tf_op jit(solution)/shard_map/prep/pallas_call | solution.py:293
  2.4 9.0 %all-to-all-start = ((bf16[8,144,128]{2,1,0:T(8,128)(2,1)}), bf16[8,144,128]{2,1,0:T(8,128)(2,1)S(1)}, u32[]{:S(2)}, u32[]{:S(2)}) async-start(bf16[8,144,128]{2,1,0:T(8,128)(2,1)} %prep.1), calls=%async_computation | async-start | bytes 589824 | tf_op jit(solution)/shard_map/all_to_all | solution.py:536
  11.4 1.0 %constant_dynamic-slice_fusion = bf16[8,128,128]{2,1,0:T(8,128)(2,1)S(1)} fusion(bf16[16,128,128]{2,1,0:T(8,128)(2,1)} %tomo_ref.3, s32[]{:T(128)S(6)} %select_n.39), kind=kLoop, calls=%fused_computation.5 | loop fusion | bytes 524292 | tf_op jit(solution)/shard_map/dynamic_slice | solution.py:539
  12.4 1.3 %collective-permute-start.5 = (bf16[8,128,128]{2,1,0:T(8,128)(2,1)S(1)}, bf16[8,128,128]{2,1,0:T(8,128)(2,1)S(1)}, u32[]{:S(2)}, u32[]{:S(2)}) collective-permute-start(bf16[8,128,128]{2,1,0:T(8,128)(2,1)S(1)} %constant_dynamic-slice_fusion), channel_id=1, source_target_pairs={{4,0},{8,4},{12,8},{16,12},{20,16},{24,20},{28,24},{32,28},{36,32}... | collective-permute-start | bytes 786440 | tf_op jit(solution)/shard_map/ppermute | solution.py:500
  13.7 1.3 %collective-permute-start.6 = (bf16[8,128,128]{2,1,0:T(8,128)(2,1)S(1)}, bf16[8,128,128]{2,1,0:T(8,128)(2,1)S(1)}, u32[]{:S(2)}, u32[]{:S(2)}) collective-permute-start(bf16[8,128,128]{2,1,0:T(8,128)(2,1)S(1)} %constant_dynamic-slice_fusion), channel_id=1, source_target_pairs={{8,0},{12,4},{16,8},{20,12},{24,16},{28,20},{32,24},{36,28},{40,32... | collective-permute-start | bytes 786440 | tf_op jit(solution)/shard_map/ppermute | solution.py:500
  15.7 7.0 %all-to-all-done = bf16[8,144,128]{2,1,0:T(8,128)(2,1)S(1)} async-done(((bf16[8,144,128]{2,1,0:T(8,128)(2,1)}), bf16[8,144,128]{2,1,0:T(8,128)(2,1)S(1)}, u32[]{:S(2)}, u32[]{:S(2)}) %all-to-all-start) | async-done | bytes 294944 | tf_op jit(solution)/shard_map/all_to_all | solution.py:536
  22.7 2.9 %collective-permute-start = (bf16[144,128]{1,0:T(8,128)(2,1)S(1)}, bf16[144,128]{1,0:T(8,128)(2,1)S(1)}, u32[]{:S(2)}, u32[]{:S(2)}) collective-permute-start(bf16[144,128]{1,0:T(8,128)(2,1)S(1)} %dynamic-slice_bitcast_fusion), channel_id=1, source_target_pairs={{0,16},{2,18},{4,20},{6,22},{8,24},{10,26},{12,28},{14,30},{16,0},... | collective-permute-start | bytes 110600 | tf_op jit(solution)/shard_map/ppermute | solution.py:520
  25.6 0.0 collective-permute-done.5
  25.6 0.0 collective-permute-done.6
  25.6 0.1 pad_maximum_fusion.own_ref
  25.7 2.6 %collective-permute-start.7 = (bf16[2,8,128,128]{3,2,1,0:T(8,128)(2,1)S(1)}, bf16[2,8,128,128]{3,2,1,0:T(8,128)(2,1)S(1)}, u32[]{:S(2)}, u32[]{:S(2)}) collective-permute-start(bf16[2,8,128,128]{3,2,1,0:T(8,128)(2,1)S(1)} %pad_maximum_fusion.own_ref), channel_id=1, source_target_pairs={{0,1},{1,0},{2,3},{3,2},{4,5},{5,4},{6,7},{7,6},{8,9},{9,8},{10,11... | collective-permute-start | bytes 1572872 | tf_op jit(solution)/shard_map/ppermute | solution.py:504
  28.3 0.0 collective-permute-done
  28.3 4.0 %collective-permute-start.1 = (bf16[144,128]{1,0:T(8,128)(2,1)S(1)}, bf16[144,128]{1,0:T(8,128)(2,1)S(1)}, u32[]{:S(2)}, u32[]{:S(2)}) collective-permute-start(bf16[144,128]{1,0:T(8,128)(2,1)S(1)} %broadcast_select_fusion), channel_id=1, source_target_pairs={{0,6},{2,4},{4,2},{6,0},{8,14},{10,12},{12,10},{14,8},{16,22},{18,... | collective-permute-start | bytes 110600 | tf_op jit(solution)/shard_map/ppermute | solution.py:520
  32.4 2.4 %collective-permute-start.2 = (bf16[144,128]{1,0:T(8,128)(2,1)S(1)}, bf16[144,128]{1,0:T(8,128)(2,1)S(1)}, u32[]{:S(2)}, u32[]{:S(2)}) collective-permute-start(bf16[144,128]{1,0:T(8,128)(2,1)S(1)} %broadcast_select_fusion), channel_id=1, source_target_pairs={{0,8},{2,10},{4,12},{6,14},{8,16},{10,18},{12,20},{14,22},{16,24},... | collective-permute-start | bytes 110600 | tf_op jit(solution)/shard_map/ppermute | solution.py:520
  34.7 0.0 collective-permute-start.3
  34.8 0.0 collective-permute-done.1.across_ref
  34.8 5.1 %collective-permute-done.2 = bf16[144,128]{1,0:T(8,128)(2,1)S(1)} collective-permute-done((bf16[144,128]{1,0:T(8,128)(2,1)S(1)}, bf16[144,128]{1,0:T(8,128)(2,1)S(1)}, u32[]{:S(2)}, u32[]{:S(2)}) %collective-permute-start.2) | collective-permute-done | bytes 36896 | tf_op jit(solution)/shard_map/ppermute | solution.py:520
  39.8 1.4 %collective-permute-done.3 = bf16[144,128]{1,0:T(8,128)(2,1)S(1)} collective-permute-done((bf16[144,128]{1,0:T(8,128)(2,1)S(1)}, bf16[144,128]{1,0:T(8,128)(2,1)S(1)}, u32[]{:S(2)}, u32[]{:S(2)}) %collective-permute-start.3) | collective-permute-done | bytes 36896 | tf_op jit(solution)/shard_map/ppermute | solution.py:520
  41.2 0.0 copy-start.1
  41.2 0.0 copy-start.2
  41.2 2.0 %collective-permute-start.4 = (bf16[144,128]{1,0:T(8,128)(2,1)S(1)}, bf16[144,128]{1,0:T(8,128)(2,1)S(1)}, u32[]{:S(2)}, u32[]{:S(2)}) collective-permute-start(bf16[144,128]{1,0:T(8,128)(2,1)S(1)} %select_select_fusion.own_ref), channel_id=1, source_target_pairs={{0,1},{1,0},{2,3},{3,2},{4,5},{5,4},{6,7},{7,6},{8,9},{9,8},{10,11... | collective-permute-start | bytes 110600 | tf_op jit(solution)/shard_map/ppermute | solution.py:504
  43.2 0.0 collective-permute-done.7.other_ref
  43.2 0.0 copy-done.4
  43.2 0.0 copy-done
  43.2 3.2 %factor.1.factor_ref = f32[16,128,128]{2,1,0:T(8,128)S(1)} custom-call(s32[1]{0:T(128)} %bitcast.core_ref, bf16[16,128,128]{2,1,0:T(8,128)(2,1)S(1)} %copy-done, bf16[2,8,128,128]{3,2,1,0:T(8,128)(2,1)S(1)} %pad_maximum_fusion.own_ref, bf16[2,8,128,128]{3,2,1,0:T(8,128)(2,1)S(1)} %collective-permute-done.7.other_ref, bf16[384,128]{1,0:T(8,128)(2,1)S(1)} %copy-done.4), custom_call_target="tpu_custom_call" | custom-call | flops 4000000000 | bytes 6000000 | tf_op jit(solution)/shard_map/factor/pallas_call | solution.py:266
  46.4 0.0 copy-done.1
  46.4 0.0 copy-done.2
  46.4 0.0 copy-start.3
  46.5 0.0 copy-start.5
  46.5 3.4 %spectrum.1.spec_ref = bf16[13,256,256]{2,1,0:T(8,128)(2,1)S(1)} custom-call(s32[1]{0:T(128)} %bitcast.core_ref, bf16[16,128,128]{2,1,0:T(8,128)(2,1)S(1)} %copy-done, bf16[2,8,128,128]{3,2,1,0:T(8,128)(2,1)S(1)} %pad_maximum_fusion.own_ref, bf16[2,8,128,128]{3,2,1,0:T(8,128)(2,1)S(1)} %collective-permute-done.7.other_ref, bf16[256,256]{1,0:T(8,128)(2,1)S(1)} %copy-done.1, ...), custom_call_target="tpu_custom_call" | custom-call | flops 4000000000 | bytes 6000000 | tf_op jit(solution)/shard_map/spectrum/pallas_call | solution.py:248
  49.8 0.0 collective-permute-done.4.other_ref
  49.9 0.0 copy-done.3
  49.9 0.0 copy-done.5
  49.9 0.0 copy-start.6
  49.9 8.4 %match.1 = bf16[16,128,128]{2,1,0:T(8,128)(2,1)S(1)} custom-call(s32[1]{0:T(128)} %bitcast.core_ref, s32[1]{0:T(128)} %bitcast.13.orient_ref, bf16[144,128]{1,0:T(8,128)(2,1)S(1)} %collective-permute-done.1.across_ref, bf16[144,128]{1,0:T(8,128)(2,1)S(1)} %select_select_fusion.own_ref, bf16[144,128]{1,0:T(8,128)(2,1)S(1)} %collective-permute-done.4.other_ref, ...), custom_call_target="tpu_custom_call" | custom-call | flops 8000000000 | bytes 6000000 | tf_op jit(solution)/shard_map/match/pallas_call | solution.py:474
  58.3 0.1 collective-permute-start.8
  58.4 0.0 copy-done.6
  58.4 1.9 %collective-permute-done.8 = bf16[16,128,128]{2,1,0:T(8,128)(2,1)S(1)} collective-permute-done((bf16[16,128,128]{2,1,0:T(8,128)(2,1)S(1)}, bf16[16,128,128]{2,1,0:T(8,128)(2,1)S(1)}, u32[]{:S(2)}, u32[]{:S(2)}) %collective-permute-start.8) | collective-permute-done | bytes 524320 | tf_op jit(solution)/shard_map/ppermute | solution.py:504
  60.3 1.1 %convert_multiply_fusion = f32[16,128,128]{2,1,0:T(8,128)} fusion(f32[16]{0:T(128)S(1)} %convert_element_type.27, bf16[16,128,128]{2,1,0:T(8,128)(2,1)S(1)} %match.1, bf16[16,128,128]{2,1,0:T(8,128)(2,1)S(1)} %collective-permute-done.8), kind=kLoop, calls=%fused_computation | loop fusion | flops 786432 | bytes 2097216 | tf_op jit(solution)/shard_map/mul | solution.py:560
  (4 shorter events, 0.0 us)
Async XLA Ops:
  0.0 43.2 %copy-start.4 = (bf16[384,128]{1,0:T(8,128)(2,1)S(1)}, bf16[384,128]{1,0:T(8,128)(2,1)}, u32[]{:S(2)}) copy-start(bf16[384,128]{1,0:T(8,128)(2,1)} %constant.63.band_ref) | copy-start | bytes 294916
  0.0 43.2 %copy-start = (bf16[16,128,128]{2,1,0:T(8,128)(2,1)S(1)}, bf16[16,128,128]{2,1,0:T(8,128)(2,1)}, u32[]{:S(2)}) copy-start(bf16[16,128,128]{2,1,0:T(8,128)(2,1)} %tomo_ref.3) | copy-start | bytes 1572868
  2.4 20.3 %all-to-all-start = ((bf16[8,144,128]{2,1,0:T(8,128)(2,1)}), bf16[8,144,128]{2,1,0:T(8,128)(2,1)S(1)}, u32[]{:S(2)}, u32[]{:S(2)}) async-start(bf16[8,144,128]{2,1,0:T(8,128)(2,1)} %prep.1), calls=%async_computation | async-start | bytes 589824 | tf_op jit(solution)/shard_map/all_to_all | solution.py:536
  12.4 13.2 %collective-permute-start.5 = (bf16[8,128,128]{2,1,0:T(8,128)(2,1)S(1)}, bf16[8,128,128]{2,1,0:T(8,128)(2,1)S(1)}, u32[]{:S(2)}, u32[]{:S(2)}) collective-permute-start(bf16[8,128,128]{2,1,0:T(8,128)(2,1)S(1)} %constant_dynamic-slice_fusion), channel_id=1, source_target_pairs={{4,0},{8,4},{12,8},{16,12},{20,16},{24,20},{28,24},{32,28},{36,32}... | collective-permute-start | bytes 786440 | tf_op jit(solution)/shard_map/ppermute | solution.py:500
  13.7 11.9 %collective-permute-start.6 = (bf16[8,128,128]{2,1,0:T(8,128)(2,1)S(1)}, bf16[8,128,128]{2,1,0:T(8,128)(2,1)S(1)}, u32[]{:S(2)}, u32[]{:S(2)}) collective-permute-start(bf16[8,128,128]{2,1,0:T(8,128)(2,1)S(1)} %constant_dynamic-slice_fusion), channel_id=1, source_target_pairs={{8,0},{12,4},{16,8},{20,12},{24,16},{28,20},{32,24},{36,28},{40,32... | collective-permute-start | bytes 786440 | tf_op jit(solution)/shard_map/ppermute | solution.py:500
  22.7 5.6 %collective-permute-start = (bf16[144,128]{1,0:T(8,128)(2,1)S(1)}, bf16[144,128]{1,0:T(8,128)(2,1)S(1)}, u32[]{:S(2)}, u32[]{:S(2)}) collective-permute-start(bf16[144,128]{1,0:T(8,128)(2,1)S(1)} %dynamic-slice_bitcast_fusion), channel_id=1, source_target_pairs={{0,16},{2,18},{4,20},{6,22},{8,24},{10,26},{12,28},{14,30},{16,0},... | collective-permute-start | bytes 110600 | tf_op jit(solution)/shard_map/ppermute | solution.py:520
  25.7 17.5 %collective-permute-start.7 = (bf16[2,8,128,128]{3,2,1,0:T(8,128)(2,1)S(1)}, bf16[2,8,128,128]{3,2,1,0:T(8,128)(2,1)S(1)}, u32[]{:S(2)}, u32[]{:S(2)}) collective-permute-start(bf16[2,8,128,128]{3,2,1,0:T(8,128)(2,1)S(1)} %pad_maximum_fusion.own_ref), channel_id=1, source_target_pairs={{0,1},{1,0},{2,3},{3,2},{4,5},{5,4},{6,7},{7,6},{8,9},{9,8},{10,11... | collective-permute-start | bytes 1572872 | tf_op jit(solution)/shard_map/ppermute | solution.py:504
  28.3 6.4 %collective-permute-start.1 = (bf16[144,128]{1,0:T(8,128)(2,1)S(1)}, bf16[144,128]{1,0:T(8,128)(2,1)S(1)}, u32[]{:S(2)}, u32[]{:S(2)}) collective-permute-start(bf16[144,128]{1,0:T(8,128)(2,1)S(1)} %broadcast_select_fusion), channel_id=1, source_target_pairs={{0,6},{2,4},{4,2},{6,0},{8,14},{10,12},{12,10},{14,8},{16,22},{18,... | collective-permute-start | bytes 110600 | tf_op jit(solution)/shard_map/ppermute | solution.py:520
  32.4 7.5 %collective-permute-start.2 = (bf16[144,128]{1,0:T(8,128)(2,1)S(1)}, bf16[144,128]{1,0:T(8,128)(2,1)S(1)}, u32[]{:S(2)}, u32[]{:S(2)}) collective-permute-start(bf16[144,128]{1,0:T(8,128)(2,1)S(1)} %broadcast_select_fusion), channel_id=1, source_target_pairs={{0,8},{2,10},{4,12},{6,14},{8,16},{10,18},{12,20},{14,22},{16,24},... | collective-permute-start | bytes 110600 | tf_op jit(solution)/shard_map/ppermute | solution.py:520
  34.7 6.5 %collective-permute-start.3 = (bf16[144,128]{1,0:T(8,128)(2,1)S(1)}, bf16[144,128]{1,0:T(8,128)(2,1)S(1)}, u32[]{:S(2)}, u32[]{:S(2)}) collective-permute-start(bf16[144,128]{1,0:T(8,128)(2,1)S(1)} %broadcast_select_fusion), channel_id=1, source_target_pairs={{0,14},{2,12},{4,10},{6,8},{8,22},{10,20},{12,18},{14,16},{16,30},... | collective-permute-start | bytes 110600 | tf_op jit(solution)/shard_map/ppermute | solution.py:520
  41.2 5.2 %copy-start.1 = (bf16[256,256]{1,0:T(8,128)(2,1)S(1)}, bf16[256,256]{1,0:T(8,128)(2,1)}, u32[]{:S(2)}) copy-start(bf16[256,256]{1,0:T(8,128)(2,1)} %constant.61.first_ref) | copy-start | bytes 393220
  41.2 5.2 %copy-start.2 = (bf16[256,256]{1,0:T(8,128)(2,1)S(1)}, bf16[256,256]{1,0:T(8,128)(2,1)}, u32[]{:S(2)}) copy-start(bf16[256,256]{1,0:T(8,128)(2,1)} %constant.62.second_ref) | copy-start | bytes 393220
  41.2 8.6 %collective-permute-start.4 = (bf16[144,128]{1,0:T(8,128)(2,1)S(1)}, bf16[144,128]{1,0:T(8,128)(2,1)S(1)}, u32[]{:S(2)}, u32[]{:S(2)}) collective-permute-start(bf16[144,128]{1,0:T(8,128)(2,1)S(1)} %select_select_fusion.own_ref), channel_id=1, source_target_pairs={{0,1},{1,0},{2,3},{3,2},{4,5},{5,4},{6,7},{7,6},{8,9},{9,8},{10,11... | collective-permute-start | bytes 110600 | tf_op jit(solution)/shard_map/ppermute | solution.py:504
  46.4 3.4 %copy-start.3 = (bf16[2,256,64]{2,1,0:T(8,128)(2,1)S(1)}, bf16[2,256,64]{2,1,0:T(8,128)(2,1)}, u32[]{:S(2)}) copy-start(bf16[2,256,64]{2,1,0:T(8,128)(2,1)} %constant.65.small_y_ref) | copy-start | bytes 196612
  46.5 3.4 %copy-start.5 = (bf16[2,64,256]{2,1,0:T(8,128)(2,1)S(1)}, bf16[2,64,256]{2,1,0:T(8,128)(2,1)}, u32[]{:S(2)}) copy-start(bf16[2,64,256]{2,1,0:T(8,128)(2,1)} %constant.64.small_z_ref) | copy-start | bytes 196612
  49.9 8.5 %copy-start.6 = (s32[16]{0:T(128)S(1)}, s32[16]{0:T(128)}, u32[]{:S(2)}) copy-start(s32[16]{0:T(128)} %param.14) | copy-start | bytes 196
  58.3 2.0 %collective-permute-start.8 = (bf16[16,128,128]{2,1,0:T(8,128)(2,1)S(1)}, bf16[16,128,128]{2,1,0:T(8,128)(2,1)S(1)}, u32[]{:S(2)}, u32[]{:S(2)}) collective-permute-start(bf16[16,128,128]{2,1,0:T(8,128)(2,1)S(1)} %match.1), channel_id=1, source_target_pairs={{0,1},{1,0},{2,3},{3,2},{4,5},{5,4},{6,7},{7,6},{8,9},{9,8},{10,11... | collective-permute-start | bytes 1572872 | tf_op jit(solution)/shard_map/ppermute | solution.py:504
